TPU v7x, 32 devices: a whole 2x2x4 slice. The times are simulated.
32 devices in a mesh: band: 4 (over y, x), img: 8 (over z, core).
Axes of the slice: x: 2, y: 2, z: 4, core: 2. Of those that a mesh axis runs over, the one named last changes fastest.
Arguments:
- images: bfloat16 [4, 128, 3328], P('band', 'img'), may hold values from -12 to 12
- references: bfloat16 [4, 32, 3328], P('band', 'img'), may hold values from -0.08 to 0.08
- noise_weight: float32 [4, 1664], P('band'), may hold values from 0.5 to 4
- masks: int32 [4, 16, 8, 49], P('band', 'img'), may hold values from 0 to 1, as said below
Outputs:
- weighted_sums: float32 [4, 32, 3328], P('band', 'img')
- weight_totals: float32 [32], P('img')
Inputs may be any that keep to these rules, and one draw needn't show every extreme that they name: `masks`: each entry is 0 or 1; translation number 49 // 2 is kept in every band, image block and orientation block.
All inputs are finite; a program needn't handle non-finite values.
Results may differ from a plain program's by a relative error of at most 0.0065.
Values may be sent and summed in bfloat16 or wider, within the bound.
No kernel may reach another device: no remote copies, remote signals or barrier semaphores. Data moves between devices by JAX's collectives and lax.ppermute only.
A program may use at most 64 MiB of HBM per device.

v0:
```python
import math
import jax
import jax.numpy as jnp
from jax import lax
from jax.sharding import PartitionSpec as P

BOX = 256
SIDE = 7
IMG_BLOCK = 8
PENALTY = 10000.0


def shift_angles(band, coef):
    index = jnp.arange(coef, dtype=jnp.int32)
    freq_x = (index * 37 + band * 11) % 257 - 128
    freq_y = (index * 61 + band * 29) % 129
    shift_ids = jnp.arange(SIDE * SIDE, dtype=jnp.int32)
    move_x = shift_ids // SIDE - SIDE // 2
    move_y = shift_ids % SIDE - SIDE // 2
    phase = (move_x[:, None] * freq_x[None, :] + move_y[:, None] * freq_y[None, :]).astype(
        jnp.float32
    )
    angle = phase * (2.0 * math.pi / BOX)
    return (jnp.cos(angle), jnp.sin(angle))


def align(pictures, cosine, sine):
    coef = cosine.shape[1]
    real = pictures[:, :coef].astype(jnp.float32)[:, None, :]
    imag = pictures[:, coef:].astype(jnp.float32)[:, None, :]
    out_real = real * cosine[None] - imag * sine[None]
    out_imag = real * sine[None] + imag * cosine[None]
    joined = jnp.concatenate([out_real, out_imag], axis=2).astype(jnp.bfloat16)
    return joined.reshape(pictures.shape[0] * cosine.shape[0], 2 * coef)


def prepare(projections, weight):
    doubled = jnp.concatenate([weight, weight])
    values = projections.astype(jnp.float32)
    weighted = (values * doubled[None, :]).astype(jnp.bfloat16)
    norms = jnp.sum(values * values * doubled[None, :], axis=1)
    return (weighted, norms)


def penalty(mask_block, img_block, orient_dev):
    blocks, owners, shift_count = mask_block.shape
    dropped = PENALTY * (1 - mask_block).astype(jnp.float32)
    dropped = jnp.transpose(dropped, (0, 2, 1))
    dropped = jnp.broadcast_to(
        dropped[:, None, :, :, None], (blocks, img_block, shift_count, owners, orient_dev)
    )
    return dropped.reshape(blocks * img_block * shift_count, owners * orient_dev)


def band_term(aligned, weighted, norms, dropped):
    cross = lax.dot_general(
        aligned, weighted, (((1,), (1,)), ((), ())), preferred_element_type=jnp.float32
    )
    return cross - 0.5 * norms[None, :] - dropped


def posterior(total, count):
    grid = total.reshape(count, -1)
    peak = jnp.max(grid, axis=1, keepdims=True)
    raised = jnp.exp(grid - peak)
    return (raised / jnp.sum(raised, axis=1, keepdims=True)).reshape(total.shape)


def combine_bands(partial_score):
    total = lax.psum(partial_score, "band")
    return total


def per_device(images, references, noise_weight, masks):
    band_index = lax.axis_index("band")
    coef = noise_weight.shape[1]
    cosine, sine = shift_angles(band_index, coef)
    weight = noise_weight[0]
    owned_refs = references[0]
    owned = owned_refs.shape[0]
    local_images = images[0]
    count = local_images.shape[0]
    aligned = align(local_images, cosine, sine)
    dropped = penalty(masks[0], IMG_BLOCK, owned)
    weighted, norms = prepare(lax.all_gather(references, "img", axis=1, tiled=True)[0], weight)
    partial_score = band_term(aligned, weighted, norms, dropped)
    score = combine_bands(partial_score)
    prob = posterior(score, count)
    post = prob.astype(jnp.bfloat16)
    totals = jnp.sum(prob, axis=0)
    sums = lax.dot_general(
        post, aligned, (((0,), (0,)), ((), ())), preferred_element_type=jnp.float32
    )
    mine_sums, mine_totals = (
        lax.psum_scatter(sums, "img", scatter_dimension=0, tiled=True),
        lax.psum_scatter(totals, "img", scatter_dimension=0, tiled=True),
    )
    return (mine_sums[None], mine_totals)


def solution(mesh):
    in_specs = (
        P("band", "img", None),
        P("band", "img", None),
        P("band", None),
        P("band", "img", None, None),
    )
    out_specs = (P("band", "img", None), P("img"))
    return jax.shard_map(
        per_device, mesh=mesh, in_specs=in_specs, out_specs=out_specs, check_vma=False
    )
```

profile of v0, /device:TPU:0, one launch (start us, length us, event | category | flops | bytes accessed | tf_op | source)
XLA Modules:
  0.0 160.8 jit_solution(395642710302518891)
XLA Ops:
  7.2 0.0 all-reduce.5.cloned.1.call-start
  7.2 0.9 slice_convert_fusion.1
  8.1 1.4 fusion.5
  9.5 3.3 %add_convert_fusion = (bf16[16,49,1664]{2,1,0:T(8,128)(2,1)S(1)}, bf16[16,49,1664]{2,1,0:T(8,128)(2,1)}) fusion(f32[49,1664]{1,0:T(8,128)S(1)} %get-tuple-element.7, f32[16,1664]{1,0:T(8,128)S(1)} %get-tuple-element.5, f32[49,1664]{1,0:T(8,128)S(1)} %get-tuple-element.6, f32[16,1664]{1,0:T(8,128)S(1)} %get-tuple-element.4), kind=kLoop, calls=%fused_computation | loop fusion | flops 10436608 | bytes 6083584 | tf_op jit(solution)/shard_map/convert.3
  12.9 3.3 %sub.60 = bf16[784,1664]{1,0:T(8,128)(2,1)} reshape(bf16[16,49,1664]{2,1,0:T(8,128)(2,1)} %get-tuple-element.3) | data formatting | bytes 5218304 | tf_op jit(solution)/shard_map/sub | solution.py:31
  16.2 0.0 copy-start.1
  16.2 0.0 copy-start.3
  16.2 0.0 copy-start.2
  16.2 3.5 %constant_dynamic-update-slice_fusion.1 = bf16[784,3328]{1,0:T(8,128)(2,1)} fusion(bf16[784,1664]{1,0:T(8,128)(2,1)} %sub.60), kind=kLoop, calls=%fused_computation.36 | loop fusion | bytes 5218304
  19.7 1.9 %add.100 = bf16[784,1664]{1,0:T(8,128)(2,1)} reshape(bf16[16,49,1664]{2,1,0:T(8,128)(2,1)S(1)} %get-tuple-element.2) | data formatting | bytes 5218304 | tf_op jit(solution)/shard_map/add | solution.py:32
  21.6 0.0 copy-done.1
  21.6 16.3 %all_gather.3 = bf16[1,32,3328]{2,0,1:T(2,128)(2,1)S(1)} all-gather(bf16[1,4,3328]{2,0,1:T(2,128)(2,1)S(1)} %copy.10), channel_id=1, replica_groups=mesh['band'=4,'img'=8] {'img'}, dimensions={1}, use_global_device_ids=true | all-gather | bytes 239616 | tf_op jit(solution)/shard_map/all_gather | solution.py:85
  38.0 0.4 convert_element_type.42
  38.4 0.0 copy-done.3
  38.5 0.2 fusion.3
  38.6 0.0 copy-done.2
  38.7 0.1 reshape.205
  38.9 3.5 %constant_dynamic-update-slice_fusion = bf16[784,3328]{1,0:T(8,128)(2,1)} fusion(bf16[784,3328]{1,0:T(8,128)(2,1)} %constant_dynamic-update-slice_fusion.1, bf16[784,1664]{1,0:T(8,128)(2,1)} %add.100), kind=kLoop, calls=%fused_computation.35 | loop fusion | bytes 5218304 | tf_op jit(solution)/shard_map/concatenate | solution.py:33
  42.3 4.8 %fusion = f32[784,32]{0,1:T(8,128)} fusion(f32[784,32]{0,1:T(8,128)S(1)} %reshape.205, bf16[784,3328]{1,0:T(8,128)(2,1)} %constant_dynamic-update-slice_fusion, f32[1,32,3328]{2,0,1:T(1,128)S(1)} %convert_element_type.42, f32[3328]{0:T(1024)S(1)} %pad_maximum_fusion, f32[32]{0:T(128)S(1)} %broadcast_multiply_fusion), kind=kOutput, calls=%fused_computation.3 | convolution fusion | flops 167248896 | bytes 5858432 | tf_op jit(solution)/shard_map/dot_general | solution.py:56
  47.1 0.0 copy-start.4
  47.1 0.0 all-reduce.5.cloned.1.call-update
  47.1 0.0 all-reduce.7.cloned.1.call-start
  47.2 42.6 %all-reduce.5.cloned.1.call-done = f32[784,32]{0,1:T(8,128)} async-done(((f32[784,32]{0,1:T(8,128)}), f32[784,32]{0,1:T(8,128)}) %all-reduce.5.cloned.1.call-update) | async-done | bytes 100368 | tf_op jit(solution)/shard_map/psum | solution.py:70
  89.8 0.0 copy-start
  89.8 1.0 reduce_max.10
  90.8 0.1 reduce_max.14
  90.9 0.1 reduce_max.18
  91.0 0.1 sub.66
  91.1 0.1 sub.67
  91.2 0.9 fusion.9
  92.1 0.1 reduce_sum.36
  92.2 0.1 reduce_sum.37
  92.3 0.1 div.24
  92.4 0.1 div.25
  92.5 4.3 %fusion.10 = f32[32,3328]{1,0:T(8,128)} fusion(bf16[784,3328]{1,0:T(8,128)(2,1)} %constant_dynamic-update-slice_fusion, f32[784,32]{0,1:T(8,128)} %all-reduce.5.cloned.1.call-done, f32[784]{0:T(1024)S(1)} %div.25, f32[784]{0:T(1024)S(1)} %sub.67), kind=kOutput, calls=%fused_computation.16 | convolution fusion | flops 167060992 | bytes 5750912 | tf_op jit(solution)/shard_map/dot_general | solution.py:91
  96.8 0.0 all-reduce.7.cloned.1.call-update
  96.8 0.0 copy-done.4
  96.8 0.6 dynamic-slice
  98.0 0.0 copy-done
  98.0 0.1 fusion.12
  98.2 16.0 %all-reduce.1 = f32[32]{0:T(128)S(1)} all-reduce(f32[32]{0:T(128)S(1)} %fusion.12), channel_id=3, replica_groups=mesh['band'=4,'img'=8] {'img'}, use_global_device_ids=true, to_apply=%region_8.9.clone | all-reduce | flops 32 | bytes 256
  114.2 0.6 dynamic-slice.3
  114.8 37.6 %all-reduce.7.cloned.1.call-done = f32[32,3328]{1,0:T(8,128)} async-done(((f32[32,3328]{1,0:T(8,128)}), f32[32,3328]{1,0:T(8,128)}) %all-reduce.7.cloned.1.call-update) | async-done | bytes 426000
  152.4 1.5 dynamic-slice_bitcast_fusion
  (9 shorter events, 0.1 us)
Async XLA Ops:
  7.2 82.7 %all-reduce.5.cloned.1.call-start = ((), (), s32[]{:S(2)}) async-start(), calls=%async_computation | async-start | bytes 229376 | tf_op jit(solution)/shard_map/psum | solution.py:70
  16.2 5.4 %copy-start.1 = (bf16[1,4,3328]{2,1,0:T(4,128)(2,1)S(1)}, bf16[1,4,3328]{2,1,0:T(4,128)(2,1)}, u32[]{:S(2)}) copy-start(bf16[1,4,3328]{2,1,0:T(4,128)(2,1)} %param.5) | copy-start | bytes 79876
  16.2 22.2 %copy-start.3 = (f32[1,1664]{1,0:T(1,128)S(1)}, f32[1,1664]{1,0:T(1,128)}, u32[]{:S(2)}) copy-start(f32[1,1664]{1,0:T(1,128)} %param.6) | copy-start | bytes 19972
  16.2 22.5 %copy-start.2 = (s32[1,2,8,49]{3,2,1,0:T(8,128)S(1)}, s32[1,2,8,49]{3,2,1,0:T(8,128)}, u32[]{:S(2)}) copy-start(s32[1,2,8,49]{3,2,1,0:T(8,128)} %param.7) | copy-start | bytes 9412
  47.1 49.7 %copy-start.4 = (u32[32]{0:T(128)S(1)}, u32[32]{0:T(128)}, u32[]{:S(2)}) copy-start(u32[32]{0:T(128)} %constant.76) | copy-start | bytes 388
  47.1 105.3 %all-reduce.7.cloned.1.call-start = ((), (), s32[]{:S(2)}) async-start(), calls=%async_computation.1 | async-start | bytes 851968
  89.8 8.2 %copy-start = (f32[784,32]{0,1:T(8,128)S(1)}, f32[784,32]{0,1:T(8,128)}, u32[]{:S(2)}) copy-start(f32[784,32]{0,1:T(8,128)} %all-reduce.5.cloned.1.call-done) | copy-start | bytes 301060
Sparse Core Ops, SparseCore 0:
  47.2 42.5 all-reduce.4
  96.9 55.4 all-reduce.6
where the time goes:
time: 161 us
  waiting for transfers between devices  80.3 us (50%)
  blocking collectives  32.4 us (20%)
  local copies, waits for them, and re-layouts  15.6 us (10%)
  between operations  14.8 us (9%)
  matrix products  9.05 us (6%)
  other arithmetic  8.56 us (5%)
    psum x1, waiting for transfers between devices, combine_bands(): total = lax.psum(partial_score, 'band')  42.6 us
    unnamed x3, waiting for transfers between devices  37.7 us
    all_gather x1, blocking collectives, per_device(): lax.all_gather(references, 'img', axis=1, tiled=True)[0]  16.3 us
    unnamed x1, blocking collectives  16 us
    dot_general x1, matrix products, band_term(): lax.dot_general(aligned, weighted, (((1,), (1,)), ((), ())), preferred_el...  4.78 us
    unnamed x14, local copies, waits for them, and re-layouts  4.7 us
    dot_general x1, matrix products, per_device(): lax.dot_general(post, aligned, (((0,), (0,)), ((), ())), preferred_elemen...  4.28 us
    concatenate x1, local copies, waits for them, and re-layouts, align(): joined = jnp.concatenate([out_real, out_imag], axis=2).astype(jnp.bfloat16)  3.46 us
  transfers between devices with their start and end apart: 2, of which 2 were waited for; matrix products, arithmetic and copies ran while one was open for 1% of the time, Pallas kernels for 0%

commit v1 on v0

--- a/solution.py
+++ b/solution.py
@@ -67,7 +67,12 @@
 
 
 def combine_bands(partial_score):
-    total = lax.psum(partial_score, "band")
+
+    def _step_on_quotas(field):
+        spare = lax.all_gather(field, "band").sum(axis=0)
+        return spare
+
+    total = _step_on_quotas(partial_score)
     return total
 
 

time: 161 us -> 125 us (0.78)
  waiting for transfers between devices: 80.3 us -> 38 us
  blocking collectives: 32.4 us -> 41.1 us
  other arithmetic: 8.56 us -> 6.72 us
    psum x1 -> x0, waiting for transfers between devices: 42.6 us -> none  [combine_bands(): total = lax.psum(partial_score, 'band')]
    all_gather x0 -> x1, blocking collectives: none -> 9.78 us  [_step_on_quotas(): spare = lax.all_gather(field, 'band').sum(axis=0)]
    unnamed x3 -> x2, waiting for transfers between devices: 37.7 us -> 38 us
    unnamed x14 -> x12, local copies, waits for them, and re-layouts: 4.7 us -> 4.71 us
  transfers between devices with their start and end apart: 2 -> 1, of which waited for: 2 -> 1; matrix products, arithmetic and copies ran while one was open for 1% -> 1% of each run, Pallas kernels for 0% -> 0%
where the time goes in v1:
time: 125 us
  blocking collectives  41.1 us (33%)
  waiting for transfers between devices  38 us (30%)
  local copies, waits for them, and re-layouts  15.6 us (12%)
  between operations  14.8 us (12%)
  matrix products  8.3 us (7%)
  other arithmetic  6.72 us (5%)
    unnamed x2, waiting for transfers between devices  38 us
    all_gather x1, blocking collectives, per_device(): lax.all_gather(references, 'img', axis=1, tiled=True)[0]  16.3 us
    unnamed x1, blocking collectives  15 us
    all_gather x1, blocking collectives, _step_on_quotas(): spare = lax.all_gather(field, 'band').sum(axis=0)  9.78 us
    unnamed x12, local copies, waits for them, and re-layouts  4.71 us
    dot_general x1, matrix products, per_device(): lax.dot_general(post, aligned, (((0,), (0,)), ((), ())), preferred_elemen...  4.21 us
    dot_general x1, matrix products, band_term(): lax.dot_general(aligned, weighted, (((1,), (1,)), ((), ())), preferred_el...  4.09 us
    concatenate x1, local copies, waits for them, and re-layouts, align(): joined = jnp.concatenate([out_real, out_imag], axis=2).astype(jnp.bfloat16)  3.46 us
  transfers between devices with their start and end apart: 1, of which 1 were waited for; matrix products, arithmetic and copies ran while one was open for 1% of the time, Pallas kernels for 0%

profile of v1, /device:TPU:0, one launch (start us, length us, event | category | flops | bytes accessed | tf_op | source)
XLA Modules:
  0.0 124.6 jit_solution(2022825206333499582)
XLA Ops:
  7.2 0.0 all-reduce.4.cloned.1.call-start
  7.2 0.9 slice_convert_fusion.1
  8.1 1.4 %fusion.6 = (f32[49,1664]{1,0:T(8,128)S(1)}, f32[49,1664]{1,0:T(8,128)S(1)}) fusion(s32[1664]{0:T(1024)S(1)} %get-tuple-element.8, s32[49]{0:T(128)S(1)} %get-tuple-element.10, s32[1664]{0:T(1024)S(1)} %get-tuple-element.9, s32[49]{0:T(128)S(1)} %get-tuple-element.11), kind=kLoop, calls=%fused_computation.12 | loop fusion | flops 407680 | bytes 665992 | tf_op jit(solution)/shard_map/cos | solution.py:24
  9.5 3.3 %add_convert_fusion = (bf16[16,49,1664]{2,1,0:T(8,128)(2,1)S(1)}, bf16[16,49,1664]{2,1,0:T(8,128)(2,1)}) fusion(f32[49,1664]{1,0:T(8,128)S(1)} %get-tuple-element.7, f32[16,1664]{1,0:T(8,128)S(1)} %get-tuple-element.5, f32[49,1664]{1,0:T(8,128)S(1)} %get-tuple-element.6, f32[16,1664]{1,0:T(8,128)S(1)} %get-tuple-element.4), kind=kLoop, calls=%fused_computation | loop fusion | flops 10436608 | bytes 6083584 | tf_op jit(solution)/shard_map/convert.3
  12.9 3.3 %sub.60 = bf16[784,1664]{1,0:T(8,128)(2,1)} reshape(bf16[16,49,1664]{2,1,0:T(8,128)(2,1)} %get-tuple-element.3) | data formatting | bytes 5218304 | tf_op jit(solution)/shard_map/sub | solution.py:31
  16.2 0.0 copy-start
  16.2 0.0 copy-start.2
  16.2 0.0 copy-start.1
  16.2 3.5 %constant_dynamic-update-slice_fusion.1 = bf16[784,3328]{1,0:T(8,128)(2,1)} fusion(bf16[784,1664]{1,0:T(8,128)(2,1)} %sub.60), kind=kLoop, calls=%fused_computation.37 | loop fusion | bytes 5218304
  19.7 1.9 %add.98 = bf16[784,1664]{1,0:T(8,128)(2,1)} reshape(bf16[16,49,1664]{2,1,0:T(8,128)(2,1)S(1)} %get-tuple-element.2) | data formatting | bytes 5218304 | tf_op jit(solution)/shard_map/add | solution.py:32
  21.6 0.0 copy-done
  21.6 16.3 %all_gather.9 = bf16[1,32,3328]{2,0,1:T(2,128)(2,1)S(1)} all-gather(bf16[1,4,3328]{2,0,1:T(2,128)(2,1)S(1)} %copy.10), channel_id=1, replica_groups=mesh['band'=4,'img'=8] {'img'}, dimensions={1}, use_global_device_ids=true | all-gather | bytes 239616 | tf_op jit(solution)/shard_map/all_gather | solution.py:90
  38.0 0.4 convert_element_type.42
  38.4 0.0 copy-done.2
  38.5 0.2 fusion.4
  38.6 0.0 copy-done.1
  38.7 0.1 reshape.205
  38.9 3.5 %constant_dynamic-update-slice_fusion = bf16[784,3328]{1,0:T(8,128)(2,1)} fusion(bf16[784,3328]{1,0:T(8,128)(2,1)} %constant_dynamic-update-slice_fusion.1, bf16[784,1664]{1,0:T(8,128)(2,1)} %add.98), kind=kLoop, calls=%fused_computation.36 | loop fusion | bytes 5218304 | tf_op jit(solution)/shard_map/concatenate | solution.py:33
  42.3 4.1 %fusion.1 = f32[1,784,32]{1,2,0:T(8,128)S(1)} fusion(f32[784,32]{0,1:T(8,128)S(1)} %reshape.205, bf16[784,3328]{1,0:T(8,128)(2,1)} %constant_dynamic-update-slice_fusion, f32[1,32,3328]{2,0,1:T(1,128)S(1)} %convert_element_type.42, f32[3328]{0:T(1024)S(1)} %pad_maximum_fusion, f32[32]{0:T(128)S(1)} %broadcast_multiply_fusion), kind=kOutput, calls=%fused_computation.4 | convolution fusion | flops 167248896 | bytes 5858432 | tf_op jit(solution)/shard_map/dot_general | solution.py:56
  46.4 0.0 copy-start.3
  46.4 9.8 %all-gather.1 = f32[4,784,32]{1,2,0:T(8,128)S(1)} all-gather(f32[1,784,32]{1,2,0:T(8,128)S(1)} %fusion.1), channel_id=2, replica_groups=mesh['band'=4,'img'=8] {'band'}, dimensions={0}, use_global_device_ids=true | all-gather | bytes 501760 | tf_op jit(solution)/shard_map/all_gather | solution.py:72
  56.3 0.1 reduce_max.14
  56.4 0.1 reduce_max.18
  56.5 0.1 sub.66
  56.5 0.1 sub.67
  56.7 0.1 reduce_sum.46
  56.8 0.1 reduce_sum.47
  56.9 0.1 div.24
  57.0 0.1 div.25
  57.1 4.2 %fusion.11 = f32[32,3328]{1,0:T(8,128)} fusion(bf16[784,3328]{1,0:T(8,128)(2,1)} %constant_dynamic-update-slice_fusion, f32[784,32]{0,1:T(8,128)S(1)} %reduce_sum.44, f32[784]{0:T(1024)S(1)} %div.25, f32[784]{0:T(1024)S(1)} %sub.67), kind=kOutput, calls=%fused_computation.17 | convolution fusion | flops 167060992 | bytes 5750912 | tf_op jit(solution)/shard_map/dot_general | solution.py:96
  61.3 0.0 all-reduce.4.cloned.1.call-update
  61.3 0.0 copy-done.3
  61.3 0.6 dynamic-slice
  62.5 0.1 fusion.13
  62.7 15.0 %all-reduce.1 = f32[32]{0:T(128)S(1)} all-reduce(f32[32]{0:T(128)S(1)} %fusion.13), channel_id=4, replica_groups=mesh['band'=4,'img'=8] {'img'}, use_global_device_ids=true, to_apply=%region_8.9.clone | all-reduce | flops 32 | bytes 256
  77.6 0.6 dynamic-slice.3
  78.2 38.0 %all-reduce.4.cloned.1.call-done = f32[32,3328]{1,0:T(8,128)} async-done(((f32[32,3328]{1,0:T(8,128)}), f32[32,3328]{1,0:T(8,128)}) %all-reduce.4.cloned.1.call-update) | async-done | bytes 426000
  116.3 1.5 %dynamic-slice_bitcast_fusion = f32[1,4,3328]{2,1,0:T(4,128)} fusion(f32[32,3328]{1,0:T(8,128)} %all-reduce.4.cloned.1.call-done, u32[]{:T(128)S(6)} %multiply.1), kind=kLoop, calls=%fused_computation.21 | loop fusion | bytes 106500 | tf_op jit(solution)/shard_map/broadcast_in_dim | solution.py:103
  (12 shorter events, 0.2 us)
Async XLA Ops:
  7.2 109.1 %all-reduce.4.cloned.1.call-start = ((), (), s32[]{:S(2)}) async-start(), calls=%async_computation | async-start | bytes 851968
  16.2 5.4 %copy-start = (bf16[1,4,3328]{2,1,0:T(4,128)(2,1)S(1)}, bf16[1,4,3328]{2,1,0:T(4,128)(2,1)}, u32[]{:S(2)}) copy-start(bf16[1,4,3328]{2,1,0:T(4,128)(2,1)} %param.5) | copy-start | bytes 79876
  16.2 22.2 %copy-start.2 = (f32[1,1664]{1,0:T(1,128)S(1)}, f32[1,1664]{1,0:T(1,128)}, u32[]{:S(2)}) copy-start(f32[1,1664]{1,0:T(1,128)} %param.6) | copy-start | bytes 19972
  16.2 22.5 %copy-start.1 = (s32[1,2,8,49]{3,2,1,0:T(8,128)S(1)}, s32[1,2,8,49]{3,2,1,0:T(8,128)}, u32[]{:S(2)}) copy-start(s32[1,2,8,49]{3,2,1,0:T(8,128)} %param.7) | copy-start | bytes 9412
  46.4 14.9 %copy-start.3 = (u32[32]{0:T(128)S(1)}, u32[32]{0:T(128)}, u32[]{:S(2)}) copy-start(u32[32]{0:T(128)} %constant.76) | copy-start | bytes 388
Sparse Core Ops, SparseCore 0:
  61.4 54.8 all-reduce.3
